TPU v7x, 128 devices: a whole 4x4x4 slice. The times are simulated.
128 devices in a mesh: pair: 2 (over core), virt: 64 (over z, y, x).
Axes of the slice: x: 4, y: 4, z: 4, core: 2. Of those that a mesh axis runs over, the one named last changes fastest.
Arguments:
- amplitudes: bfloat16 [512, 32768], P('virt', 'pair'), may hold values from -6 to 6
- integrals: bfloat16 [32768, 32768], P('virt', 'pair'), may hold values from -0.03125 to 0.03125
- cycle_integrals: bfloat16 [16384, 16384], P('pair', 'virt'), may hold values from -0.125 to 0.125
- virt_count: int32 [8], replicated, may hold values from 32 to 64, as said below
Outputs:
- ladder: bfloat16 [512, 32768], P(None, 'virt')
- cycle: bfloat16 [8192, 16384], P('pair', 'virt')
Inputs may be any that keep to these rules, and one draw needn't show every extreme that they name: `virt_count`: every irrep keeps at least half of its 64 slots; some irrep has all 64 and some has exactly half.
All inputs are finite; a program needn't handle non-finite values.
Results may differ from a plain program's by a relative error of at most 0.0049.
Values may be sent and summed in bfloat16 or wider, within the bound.
No kernel may reach another device: no remote copies, remote signals or barrier semaphores. Data moves between devices by JAX's collectives and lax.ppermute only.
A program may use at most 256 MiB of HBM per device.

v0:
```python
import jax
import jax.numpy as jnp
from jax import lax
from jax.sharding import PartitionSpec as P

VH = 64
OI = 16
OJ = 32


def irrep_sizes(virt_count, irrep_of):
    irrep_ids = jnp.arange(virt_count.shape[0], dtype=jnp.int32)
    return jnp.sum(
        jnp.where(irrep_of[:, None] == irrep_ids[None, :], virt_count[None, :], 0), axis=1
    )


def pair_mask(virt_count, first_pos, length, slot_width):
    position = first_pos + jnp.arange(length, dtype=jnp.int32)
    irrep_of = position // (slot_width * slot_width)
    slot_one = position // slot_width % slot_width
    slot_two = position % slot_width
    irrep_size = irrep_sizes(virt_count, irrep_of)
    return ((slot_one < irrep_size) & (slot_two < irrep_size)).astype(jnp.float32)


def slot_mask(virt_count, first_pos, length, slot_width):
    position = (first_pos + jnp.arange(length, dtype=jnp.int32)) % (
        virt_count.shape[0] * slot_width
    )
    irrep_of = position // slot_width
    slot_ids = position % slot_width
    return (slot_ids < irrep_sizes(virt_count, irrep_of)).astype(jnp.float32)


def body(amplitudes, integrals, cycle_integrals, virt_count):
    slot_width = VH
    irrep_total = virt_count.shape[0]
    group_width = irrep_total * slot_width
    pair_devs = lax.axis_size("pair")
    ab_count = integrals.shape[0]
    cd_count = integrals.shape[1]
    jb_count = cycle_integrals.shape[1]
    cd_first = lax.axis_index("pair") * cd_count
    ab_first = lax.axis_index("virt") * ab_count
    a_count = ab_count // slot_width
    per_irrep = slot_width * slot_width // ab_count
    masked = amplitudes * pair_mask(virt_count, cd_first, cd_count, slot_width)[None, :].astype(
        jnp.bfloat16
    )
    partial_sums = lax.dot_general(
        lax.all_gather(masked, "virt", axis=0, tiled=True),
        integrals,
        (((1,), (1,)), ((), ())),
        preferred_element_type=jnp.float32,
    )
    keep_pairs = pair_mask(virt_count, ab_first, ab_count, slot_width)[None, :]
    ladder_total = lax.psum(partial_sums, "pair")
    ladder = (ladder_total * keep_pairs).astype(jnp.bfloat16)
    keep_cols = slot_mask(virt_count, lax.axis_index("virt") * jb_count, jb_count, slot_width)[
        None, :
    ]
    pair_rows = ladder.reshape(OI, OJ, ab_count)
    k_local = OJ // pair_devs
    own_k = lax.dynamic_slice_in_dim(pair_rows, lax.axis_index("pair") * k_local, k_local, 1)[None]
    cycle_local = cycle_integrals.reshape(k_local, irrep_total, slot_width, jb_count)
    shards = lax.all_gather(own_k, "virt", axis=0, tiled=True)
    shard_count = shards.shape[0]
    irrep_ids = jnp.arange(shard_count, dtype=jnp.int32) * ab_count // (slot_width * slot_width)
    chosen = jnp.take(cycle_local, irrep_ids, axis=1)
    amp_block = shards.reshape(shard_count, OI, k_local, a_count, slot_width)
    pieces = jnp.einsum("sikac,kscj->siaj", amp_block, chosen, preferred_element_type=jnp.float32)
    full_term = jnp.transpose(
        pieces.reshape(irrep_total, per_irrep, OI, a_count, jb_count), (2, 0, 1, 3, 4)
    )
    full_term = full_term.reshape(OI * group_width, jb_count)
    summed = lax.psum_scatter(full_term, "pair", scatter_dimension=0, tiled=True)
    cycle = (summed * keep_cols).astype(jnp.bfloat16)
    return (ladder, cycle)


def solution(mesh):
    placed = (P("virt", "pair"), P("virt", "pair"), P("pair", "virt"), P())
    return jax.shard_map(
        body,
        mesh=mesh,
        in_specs=placed,
        out_specs=(P(None, "virt"), P("pair", "virt")),
        check_vma=False,
    )
```

profile of v0, /device:TPU:1, one launch (start us, length us, event | category | flops | bytes accessed | tf_op | source)
XLA Modules:
  0.0 376.8 jit_solution(9450437816914688675)
XLA Ops:
  7.2 0.0 all-gather.4.cloned.1.call-start
  7.3 0.9 select_reduce_fusion
  8.2 0.1 convert_convert_fusion
  8.3 1.7 broadcast_multiply_fusion
  10.0 0.0 all-gather.4.cloned.1.call-update
  10.0 0.0 copy-start.1
  10.0 0.0 all-reduce.2.cloned.1.call-start
  10.1 109.0 %all-gather.4.cloned.1.call-done = bf16[512,16384]{1,0:T(8,128)(2,1)} async-done(((bf16[8,16384]{1,0:T(8,128)(2,1)}), bf16[512,16384]{1,0:T(8,128)(2,1)}) %all-gather.4.cloned.1.call-update) | async-done | bytes 16777232 | tf_op jit(solution)/shard_map/all_gather | solution.py:52
  119.1 18.0 %fusion.26 = f32[512,512]{1,0:T(8,128)} fusion(bf16[512,16384]{1,0:T(8,128)(2,1)} %all-gather.4.cloned.1.call-done, bf16[512,16384]{1,0:T(8,128)(2,1)} %param.5), kind=kOutput, calls=%fused_computation.87 | convolution fusion | flops 8589934592 | bytes 34603008 | tf_op jit(solution)/shard_map/dot_general | solution.py:51
  137.1 0.0 all-reduce.2.cloned.1.call-update
  137.1 0.0 all-gather.6.cloned.1.call-start
  137.2 0.0 copy-done.1
  137.2 0.1 select_reduce_fusion.1
  137.3 25.1 %all-reduce.2.cloned.1.call-done = f32[512,512]{1,0:T(8,128)} async-done(((f32[512,512]{1,0:T(8,128)}), f32[512,512]{1,0:T(8,128)}) %all-reduce.2.cloned.1.call-update) | async-done | bytes 1048592 | tf_op jit(solution)/shard_map/psum | solution.py:58
  162.4 1.3 multiply_convert_fusion.1
  163.8 0.0 copy-start
  163.8 0.8 constant_dynamic-slice_fusion
  164.6 0.0 all-gather.6.cloned.1.call-update
  164.6 0.0 reduce-scatter.2.cloned.1.call-start
  164.7 14.7 %gather_fusion = bf16[64,16,64,256]{3,2,1,0:T(8,128)(2,1)} fusion(bf16[16,8,64,256]{3,2,1,0:T(8,128)(2,1)} %bitcast.21, s32[1024]{0:T(1024)S(1)} %pad_clamp_fusion), kind=kCustom, calls=%fused_computation | custom fusion | bytes 67109120 | tf_op jit(solution)/shard_map/jit(_take)/gather | solution.py:70
  179.4 0.0 copy-done
  179.4 92.2 %all-gather.6.cloned.1.call-done = bf16[1024,16,512]{2,1,0:T(8,128)(2,1)} async-done(((bf16[16,16,512]{2,1,0:T(8,128)(2,1)}), bf16[1024,16,512]{2,1,0:T(8,128)(2,1)}) %all-gather.6.cloned.1.call-update) | async-done | bytes 16777232 | tf_op jit(solution)/shard_map/all_gather | solution.py:67
  271.6 41.3 %reshape.281 = bf16[64,16,16,8,64]{4,3,2,1,0:T(8,128)(2,1)} reshape(bf16[1024,16,512]{2,1,0:T(8,128)(2,1)} %all-gather.6.cloned.1.call-done) | data formatting | bytes 33554432 | tf_op jit(solution)/shard_map/reshape | solution.py:71
  312.9 25.9 %fusion = f32[64,16,8,256,1]{3,2,4,1,0:T(8,128)} fusion(bf16[64,16,16,8,64]{4,3,2,1,0:T(8,128)(2,1)} %reshape.281, bf16[64,16,64,256]{3,2,1,0:T(8,128)(2,1)} %gather_fusion, pred[64]{0:T(512)(128)(4,1)S(1)} %compare_and_fusion), kind=kOutput, calls=%fused_computation.1 | convolution fusion | flops 4311744512 | bytes 58720320 | tf_op jit(solution)/shard_map/sikac,kscj->siaj/dot_general | solution.py:72
  338.8 7.9 %copy.8 = f32[16,8,8,8,256]{4,3,2,1,0:T(8,128)} copy(f32[16,8,8,8,256]{4,3,0,2,1:T(8,128)} %bitcast.23) | data formatting | bytes 16777216 | tf_op jit(solution)/shard_map/transpose | solution.py:73
  346.7 0.0 reduce-scatter.2.cloned.1.call-update
  346.8 0.1 select_reduce_fusion.2
  346.9 19.5 %reduce-scatter.2.cloned.1.call-done = f32[4096,256]{1,0:T(8,128)} async-done(((f32[8192,256]{1,0:T(8,128)}), f32[4096,256]{1,0:T(8,128)}) %reduce-scatter.2.cloned.1.call-update) | async-done | bytes 4194320 | tf_op jit(solution)/shard_map/reduce_scatter | solution.py:77
  366.4 3.8 %multiply_convert_fusion = bf16[4096,256]{1,0:T(8,128)(2,1)} fusion(f32[4096,256]{1,0:T(8,128)} %reduce-scatter.2.cloned.1.call-done, f32[256]{0:T(256)S(1)} %compare_convert_fusion), kind=kLoop, calls=%fused_computation.6 | loop fusion | flops 2097152 | bytes 6292480 | tf_op jit(solution)/shard_map/convert_element_type | solution.py:78
  (8 shorter events, 0.2 us)
Async XLA Ops:
  7.2 111.9 %all-gather.4.cloned.1.call-start = ((), (), s32[]{:S(2)}) async-start(), calls=%async_computation.1 | async-start | bytes 17039360 | tf_op jit(solution)/shard_map/all_gather | solution.py:52
  10.0 127.2 %copy-start.1 = (s32[8]{0:T(128)S(1)}, s32[8]{0:T(128)}, u32[]{:S(2)}) copy-start(s32[8]{0:T(128)} %param.7) | copy-start | bytes 100
  10.0 152.4 %all-reduce.2.cloned.1.call-start = ((), (), s32[]{:S(2)}) async-start(), calls=%async_computation.2 | async-start | bytes 2097152 | tf_op jit(solution)/shard_map/psum | solution.py:58
  137.1 134.5 %all-gather.6.cloned.1.call-start = ((), (), s32[]{:S(2)}) async-start(), calls=%async_computation.4 | async-start | bytes 17039360 | tf_op jit(solution)/shard_map/all_gather | solution.py:67
  163.8 15.6 %copy-start = (bf16[512,512]{1,0:T(8,128)(2,1)}, bf16[512,512]{1,0:T(8,128)(2,1)S(1)}, u32[]{:S(2)}) copy-start(bf16[512,512]{1,0:T(8,128)(2,1)S(1)} %multiply_convert_fusion.1) | copy-start | bytes 1572868
  164.6 201.8 %reduce-scatter.2.cloned.1.call-start = ((), (), s32[]{:S(2)}) async-start(), calls=%async_computation.3 | async-start | bytes 12582912 | tf_op jit(solution)/shard_map/reduce_scatter | solution.py:77
Sparse Core Ops, SparseCore 0:
  11.4 107.5 all-gather.3
  137.2 25.1 all-reduce.1
  166.3 105.2 all-gather.5
  346.9 19.4 reduce-scatter.1
where the time goes:
time: 378 us; the launch traced here: 377 us
  waiting for transfers between devices  246 us (65%)
  local copies, waits for them, and re-layouts  64.7 us (17%)
  matrix products  43.9 us (12%)
  between operations  13.8 us (4%)
  other arithmetic  8.2 us (2%)
    all_gather x1, waiting for transfers between devices, body(): lax.all_gather(masked, 'virt', axis=0, tiled=True)  109 us
    all_gather x1, waiting for transfers between devices, body(): shards = lax.all_gather(own_k, 'virt', axis=0, tiled=True)  92.2 us
    reshape x1, local copies, waits for them, and re-layouts, body(): amp_block = shards.reshape(shard_count, OI, k_local, a_count, slot_width)  41.3 us
    dot_general x1, matrix products, body(): jnp.einsum('sikac,kscj->siaj', amp_block, chosen, preferred_element_type=...  25.9 us
    psum x1, waiting for transfers between devices, body(): ladder_total = lax.psum(partial_sums, 'pair')  25.1 us
    reduce_scatter x1, waiting for transfers between devices, body(): lax.psum_scatter(full_term, 'pair', scatter_dimension=0, tiled=True)  19.5 us
    dot_general x1, matrix products, body(): lax.dot_general(lax.all_gather(masked, 'virt', axis=0, tiled=True), integ...  18 us
    gather x1, local copies, waits for them, and re-layouts, body(): chosen = jnp.take(cycle_local, irrep_ids, axis=1)  14.7 us
  transfers between devices with their start and end apart: 4, of which 4 were waited for; matrix products, arithmetic and copies ran while one was open for 4% of the time, Pallas kernels for 0%

commit v1 on v0

--- a/solution.py
+++ b/solution.py
@@ -49,7 +49,9 @@
         jnp.bfloat16
     )
     partial_sums = lax.dot_general(
-        lax.all_gather(masked, "virt", axis=0, tiled=True),
+        jnp.concatenate(
+            lax.all_to_all(jnp.stack([masked] * lax.axis_size("virt")), "virt", 0, 0), axis=0
+        ),
         integrals,
         (((1,), (1,)), ((), ())),
         preferred_element_type=jnp.float32,

time: 378 us -> 474 us (1.25)
  blocking collectives: 0 us -> 204 us
  waiting for transfers between devices: 246 us -> 137 us
    all_to_all x0 -> x1, blocking collectives: none -> 204 us  [body(): lax.all_to_all(jnp.stack([masked] * lax.axis_size('virt')), 'virt', 0, 0)]
    all_gather x1 -> x0, waiting for transfers between devices: 109 us -> none  [body(): lax.all_gather(masked, 'virt', axis=0, tiled=True)]
  transfers between devices with their start and end apart: 4 -> 3, of which waited for: 4 -> 3; matrix products, arithmetic and copies ran while one was open for 4% -> 3% of each run, Pallas kernels for 0% -> 0%
where the time goes in v1:
time: 474 us; the launch traced here: 473 us
  blocking collectives  204 us (43%)
  waiting for transfers between devices  137 us (29%)
  local copies, waits for them, and re-layouts  66.8 us (14%)
  matrix products  43.9 us (9%)
  between operations  13.8 us (3%)
  other arithmetic  7.5 us (2%)
    all_to_all x1, blocking collectives, body(): lax.all_to_all(jnp.stack([masked] * lax.axis_size('virt')), 'virt', 0, 0)  204 us
    all_gather x1, waiting for transfers between devices, body(): shards = lax.all_gather(own_k, 'virt', axis=0, tiled=True)  92.2 us
    reshape x1, local copies, waits for them, and re-layouts, body(): amp_block = shards.reshape(shard_count, OI, k_local, a_count, slot_width)  41.3 us
    dot_general x1, matrix products, body(): jnp.einsum('sikac,kscj->siaj', amp_block, chosen, preferred_element_type=...  25.9 us
    psum x1, waiting for transfers between devices, body(): ladder_total = lax.psum(partial_sums, 'pair')  24.9 us
    reduce_scatter x1, waiting for transfers between devices, body(): lax.psum_scatter(full_term, 'pair', scatter_dimension=0, tiled=True)  19.5 us
    dot_general x1, matrix products, body(): lax.dot_general(jnp.concatenate(lax.all_to_all(jnp.stack([masked] * lax.a...  18 us
    gather x1, local copies, waits for them, and re-layouts, body(): chosen = jnp.take(cycle_local, irrep_ids, axis=1)  14.7 us
  transfers between devices with their start and end apart: 3, of which 3 were waited for; matrix products, arithmetic and copies ran while one was open for 3% of the time, Pallas kernels for 0%

profile of v1, /device:TPU:1, one launch (start us, length us, event | category | flops | bytes accessed | tf_op | source)
XLA Modules:
  0.0 473.0 jit_solution(11148355565614744178)
XLA Ops:
  7.2 0.0 all-reduce.2.cloned.1.call-start
  7.3 0.9 select_reduce_fusion
  8.2 0.1 convert_convert_fusion
  8.3 1.0 broadcast_multiply_fusion
  9.3 2.1 stack.2
  11.4 204.1 %all_to_all.5 = bf16[64,8,16384]{2,1,0:T(8,128)(2,1)} all-to-all(bf16[64,8,16384]{2,1,0:T(8,128)(2,1)S(1)} %stack.2), channel_id=1, replica_groups=mesh['pair'=2,'virt'=64] {'virt'}, dimensions={0} | all-to-all | bytes 33554432 | tf_op jit(solution)/shard_map/all_to_all | solution.py:53
  215.5 0.0 copy-start.1
  215.5 18.0 %fusion.4 = f32[512,512]{1,0:T(8,128)} fusion(bf16[512,16384]{1,0:T(8,128)(2,1)} %param.5, bf16[64,8,16384]{2,1,0:T(8,128)(2,1)} %all_to_all.5), kind=kOutput, calls=%fused_computation.5 | convolution fusion | flops 8589934592 | bytes 34603008 | tf_op jit(solution)/shard_map/dot_general | solution.py:51
  233.5 0.0 all-reduce.2.cloned.1.call-update
  233.5 0.0 all-gather.3.cloned.1.call-start
  233.6 0.0 copy-done.1
  233.6 0.1 select_reduce_fusion.1
  233.7 24.9 %all-reduce.2.cloned.1.call-done = f32[512,512]{1,0:T(8,128)} async-done(((f32[512,512]{1,0:T(8,128)}), f32[512,512]{1,0:T(8,128)}) %all-reduce.2.cloned.1.call-update) | async-done | bytes 1048592 | tf_op jit(solution)/shard_map/psum | solution.py:60
  258.7 1.3 multiply_convert_fusion.1
  260.0 0.0 copy-start
  260.0 0.8 constant_dynamic-slice_fusion
  260.8 0.0 all-gather.3.cloned.1.call-update
  260.9 0.0 reduce-scatter.2.cloned.1.call-start
  261.0 14.7 %gather_fusion = bf16[64,16,64,256]{3,2,1,0:T(8,128)(2,1)} fusion(bf16[16,8,64,256]{3,2,1,0:T(8,128)(2,1)} %bitcast.23, s32[1024]{0:T(1024)S(1)} %pad_clamp_fusion), kind=kCustom, calls=%fused_computation | custom fusion | bytes 67109120 | tf_op jit(solution)/shard_map/jit(_take)/gather | solution.py:72
  275.6 0.0 copy-done
  275.7 92.2 %all-gather.3.cloned.1.call-done = bf16[1024,16,512]{2,1,0:T(8,128)(2,1)} async-done(((bf16[16,16,512]{2,1,0:T(8,128)(2,1)}), bf16[1024,16,512]{2,1,0:T(8,128)(2,1)}) %all-gather.3.cloned.1.call-update) | async-done | bytes 16777232 | tf_op jit(solution)/shard_map/all_gather | solution.py:69
  367.9 41.3 %reshape.287 = bf16[64,16,16,8,64]{4,3,2,1,0:T(8,128)(2,1)} reshape(bf16[1024,16,512]{2,1,0:T(8,128)(2,1)} %all-gather.3.cloned.1.call-done) | data formatting | bytes 33554432 | tf_op jit(solution)/shard_map/reshape | solution.py:73
  409.2 25.9 %fusion = f32[64,16,8,256,1]{3,2,4,1,0:T(8,128)} fusion(bf16[64,16,16,8,64]{4,3,2,1,0:T(8,128)(2,1)} %reshape.287, bf16[64,16,64,256]{3,2,1,0:T(8,128)(2,1)} %gather_fusion, pred[64]{0:T(512)(128)(4,1)S(1)} %compare_and_fusion), kind=kOutput, calls=%fused_computation.1 | convolution fusion | flops 4311744512 | bytes 58720320 | tf_op jit(solution)/shard_map/sikac,kscj->siaj/dot_general | solution.py:74
  435.1 7.9 %copy.8 = f32[16,8,8,8,256]{4,3,2,1,0:T(8,128)} copy(f32[16,8,8,8,256]{4,3,0,2,1:T(8,128)} %bitcast.25) | data formatting | bytes 16777216 | tf_op jit(solution)/shard_map/transpose | solution.py:75
  443.0 0.0 reduce-scatter.2.cloned.1.call-update
  443.0 0.1 select_reduce_fusion.2
  443.1 19.5 %reduce-scatter.2.cloned.1.call-done = f32[4096,256]{1,0:T(8,128)} async-done(((f32[8192,256]{1,0:T(8,128)}), f32[4096,256]{1,0:T(8,128)}) %reduce-scatter.2.cloned.1.call-update) | async-done | bytes 4194320 | tf_op jit(solution)/shard_map/reduce_scatter | solution.py:79
  462.6 3.8 multiply_convert_fusion
  (8 shorter events, 0.2 us)
Async XLA Ops:
  7.2 251.5 %all-reduce.2.cloned.1.call-start = ((), (), s32[]{:S(2)}) async-start(), calls=%async_computation.2 | async-start | bytes 2097152 | tf_op jit(solution)/shard_map/psum | solution.py:60
  215.5 18.1 %copy-start.1 = (s32[8]{0:T(128)S(1)}, s32[8]{0:T(128)}, u32[]{:S(2)}) copy-start(s32[8]{0:T(128)} %param.7) | copy-start | bytes 100
  233.5 134.3 %all-gather.3.cloned.1.call-start = ((), (), s32[]{:S(2)}) async-start(), calls=%async_computation.4 | async-start | bytes 17039360 | tf_op jit(solution)/shard_map/all_gather | solution.py:69
  260.0 15.6 %copy-start = (bf16[512,512]{1,0:T(8,128)(2,1)}, bf16[512,512]{1,0:T(8,128)(2,1)S(1)}, u32[]{:S(2)}) copy-start(bf16[512,512]{1,0:T(8,128)(2,1)S(1)} %multiply_convert_fusion.1) | copy-start | bytes 1572868
  260.9 201.8 %reduce-scatter.2.cloned.1.call-start = ((), (), s32[]{:S(2)}) async-start(), calls=%async_computation.3 | async-start | bytes 12582912 | tf_op jit(solution)/shard_map/reduce_scatter | solution.py:79
Sparse Core Ops, SparseCore 0:
  233.7 24.9 all-reduce.1
  262.5 105.2 all-gather.2
  443.1 19.4 reduce-scatter.1

commit v2 on v0

--- a/solution.py
+++ b/solution.py
@@ -55,7 +55,7 @@
         preferred_element_type=jnp.float32,
     )
     keep_pairs = pair_mask(virt_count, ab_first, ab_count, slot_width)[None, :]
-    ladder_total = lax.psum(partial_sums, "pair")
+    ladder_total = jnp.sum(lax.all_gather(partial_sums, "pair"), axis=0)
     ladder = (ladder_total * keep_pairs).astype(jnp.bfloat16)
     keep_cols = slot_mask(virt_count, lax.axis_index("virt") * jb_count, jb_count, slot_width)[
         None, :

time: 378 us -> 366 us (0.968)
  waiting for transfers between devices: 246 us -> 232 us
    psum x1 -> x0, waiting for transfers between devices: 25.1 us -> none  [body(): ladder_total = lax.psum(partial_sums, 'pair')]
    all_gather x0 -> x1, waiting for transfers between devices: none -> 13.2 us  [body(): ladder_total = jnp.sum(lax.all_gather(partial_sums, 'pair'), axis=0)]
where the time goes in v2:
time: 366 us; the launch traced here: 364 us
  waiting for transfers between devices  232 us (63%)
  local copies, waits for them, and re-layouts  63.9 us (17%)
  matrix products  43.9 us (12%)
  between operations  13.8 us (4%)
  other arithmetic  10.4 us (3%)
    all_gather x1, waiting for transfers between devices, body(): lax.all_gather(masked, 'virt', axis=0, tiled=True)  109 us
    all_gather x1, waiting for transfers between devices, body(): shards = lax.all_gather(own_k, 'virt', axis=0, tiled=True)  91.3 us
    reshape x1, local copies, waits for them, and re-layouts, body(): amp_block = shards.reshape(shard_count, OI, k_local, a_count, slot_width)  41.3 us
    dot_general x1, matrix products, body(): jnp.einsum('sikac,kscj->siaj', amp_block, chosen, preferred_element_type=...  25.9 us
    reduce_scatter x1, waiting for transfers between devices, body(): lax.psum_scatter(full_term, 'pair', scatter_dimension=0, tiled=True)  18.6 us
    dot_general x1, matrix products, body(): lax.dot_general(lax.all_gather(masked, 'virt', axis=0, tiled=True), integ...  18 us
    gather x1, local copies, waits for them, and re-layouts, body(): chosen = jnp.take(cycle_local, irrep_ids, axis=1)  14.7 us
    all_gather x1, waiting for transfers between devices, body(): ladder_total = jnp.sum(lax.all_gather(partial_sums, 'pair'), axis=0)  13.2 us
  transfers between devices with their start and end apart: 4, of which 4 were waited for; matrix products, arithmetic and copies ran while one was open for 4% of the time, Pallas kernels for 0%

profile of v2, /device:TPU:1, one launch (start us, length us, event | category | flops | bytes accessed | tf_op | source)
XLA Modules:
  0.0 364.5 jit_solution(6908478136303853208)
XLA Ops:
  7.2 0.0 all-gather.6.cloned.1.call-start
  7.3 0.9 select_reduce_fusion
  8.2 0.1 convert_convert_fusion
  8.3 1.7 broadcast_multiply_fusion
  10.0 0.0 all-gather.6.cloned.1.call-update
  10.0 0.0 copy-start
  10.0 0.0 all-gather.8.cloned.1.call-start
  10.1 109.0 %all-gather.6.cloned.1.call-done = bf16[512,16384]{1,0:T(8,128)(2,1)} async-done(((bf16[8,16384]{1,0:T(8,128)(2,1)}), bf16[512,16384]{1,0:T(8,128)(2,1)}) %all-gather.6.cloned.1.call-update) | async-done | bytes 16777232 | tf_op jit(solution)/shard_map/all_gather | solution.py:52
  119.1 18.0 %fusion.27 = f32[512,512]{1,0:T(8,128)} fusion(bf16[512,16384]{1,0:T(8,128)(2,1)} %all-gather.6.cloned.1.call-done, bf16[512,16384]{1,0:T(8,128)(2,1)} %param.5), kind=kOutput, calls=%fused_computation.88 | convolution fusion | flops 8589934592 | bytes 34603008 | tf_op jit(solution)/shard_map/dot_general | solution.py:51
  137.1 0.0 all-gather.8.cloned.1.call-update
  137.1 0.0 all-gather.10.cloned.1.call-start
  137.2 0.0 copy-done
  137.2 0.1 select_reduce_fusion.1
  137.3 13.2 %all-gather.8.cloned.1.call-done = f32[1024,512]{1,0:T(8,128)} async-done(((f32[512,512]{1,0:T(8,128)}), f32[1024,512]{1,0:T(8,128)}) %all-gather.8.cloned.1.call-update) | async-done | bytes 2097168 | tf_op jit(solution)/shard_map/all_gather | solution.py:58
  150.5 1.9 reduce_sum.39
  152.4 0.8 fusion.5
  153.2 0.0 all-gather.10.cloned.1.call-update
  153.2 0.0 reduce-scatter.2.cloned.1.call-start
  153.3 14.7 %gather_fusion = bf16[64,16,64,256]{3,2,1,0:T(8,128)(2,1)} fusion(bf16[16,8,64,256]{3,2,1,0:T(8,128)(2,1)} %bitcast.22, s32[1024]{0:T(1024)S(1)} %pad_clamp_fusion), kind=kCustom, calls=%fused_computation | custom fusion | bytes 67109120 | tf_op jit(solution)/shard_map/jit(_take)/gather | solution.py:70
  168.0 91.3 %all-gather.10.cloned.1.call-done = bf16[1024,16,512]{2,1,0:T(8,128)(2,1)} async-done(((bf16[16,16,512]{2,1,0:T(8,128)(2,1)}), bf16[1024,16,512]{2,1,0:T(8,128)(2,1)}) %all-gather.10.cloned.1.call-update) | async-done | bytes 16777232 | tf_op jit(solution)/shard_map/all_gather | solution.py:67
  259.3 41.3 %reshape.284 = bf16[64,16,16,8,64]{4,3,2,1,0:T(8,128)(2,1)} reshape(bf16[1024,16,512]{2,1,0:T(8,128)(2,1)} %all-gather.10.cloned.1.call-done) | data formatting | bytes 33554432 | tf_op jit(solution)/shard_map/reshape | solution.py:71
  300.6 25.9 %fusion = f32[64,16,8,256,1]{3,2,4,1,0:T(8,128)} fusion(bf16[64,16,16,8,64]{4,3,2,1,0:T(8,128)(2,1)} %reshape.284, bf16[64,16,64,256]{3,2,1,0:T(8,128)(2,1)} %gather_fusion, pred[64]{0:T(512)(128)(4,1)S(1)} %compare_and_fusion), kind=kOutput, calls=%fused_computation.1 | convolution fusion | flops 4311744512 | bytes 58720320 | tf_op jit(solution)/shard_map/sikac,kscj->siaj/dot_general | solution.py:72
  326.5 7.9 %copy.8 = f32[16,8,8,8,256]{4,3,2,1,0:T(8,128)} copy(f32[16,8,8,8,256]{4,3,0,2,1:T(8,128)} %bitcast.24) | data formatting | bytes 16777216 | tf_op jit(solution)/shard_map/transpose | solution.py:73
  334.4 0.0 reduce-scatter.2.cloned.1.call-update
  334.5 0.1 select_reduce_fusion.2
  334.6 0.9 multiply_convert_fusion.1
  335.5 18.6 %reduce-scatter.2.cloned.1.call-done = f32[4096,256]{1,0:T(8,128)} async-done(((f32[8192,256]{1,0:T(8,128)}), f32[4096,256]{1,0:T(8,128)}) %reduce-scatter.2.cloned.1.call-update) | async-done | bytes 4194320 | tf_op jit(solution)/shard_map/reduce_scatter | solution.py:77
  354.1 3.8 %multiply_convert_fusion = bf16[4096,256]{1,0:T(8,128)(2,1)} fusion(f32[4096,256]{1,0:T(8,128)} %reduce-scatter.2.cloned.1.call-done, f32[256]{0:T(256)S(1)} %compare_convert_fusion), kind=kLoop, calls=%fused_computation.6 | loop fusion | flops 2097152 | bytes 6292480 | tf_op jit(solution)/shard_map/convert_element_type | solution.py:78
  (8 shorter events, 0.2 us)
Async XLA Ops:
  7.2 111.9 %all-gather.6.cloned.1.call-start = ((), (), s32[]{:S(2)}) async-start(), calls=%async_computation.1 | async-start | bytes 17039360 | tf_op jit(solution)/shard_map/all_gather | solution.py:52
  10.0 127.2 %copy-start = (s32[8]{0:T(128)S(1)}, s32[8]{0:T(128)}, u32[]{:S(2)}) copy-start(s32[8]{0:T(128)} %param.7) | copy-start | bytes 100
  10.0 140.5 %all-gather.8.cloned.1.call-start = ((), (), s32[]{:S(2)}) async-start(), calls=%async_computation.3 | async-start | bytes 3145728 | tf_op jit(solution)/shard_map/all_gather | solution.py:58
  137.1 122.2 %all-gather.10.cloned.1.call-start = ((), (), s32[]{:S(2)}) async-start(), calls=%async_computation.4 | async-start | bytes 17039360 | tf_op jit(solution)/shard_map/all_gather | solution.py:67
  153.2 200.9 %reduce-scatter.2.cloned.1.call-start = ((), (), s32[]{:S(2)}) async-start(), calls=%async_computation.2 | async-start | bytes 12582912 | tf_op jit(solution)/shard_map/reduce_scatter | solution.py:77
Sparse Core Ops, SparseCore 0:
  11.4 107.5 all-gather.5
  137.2 13.2 all-gather.7
  154.0 105.2 all-gather.9
  334.6 19.4 reduce-scatter.1
